TPU v7x, 32 devices: a whole 2x2x4 slice. The times are simulated.
32 devices in a mesh: ckpt: 4 (over x, core), wide: 8 (over z, y).
Axes of the slice: x: 2, y: 2, z: 4, core: 2. Of those that a mesh axis runs over, the one named last changes fastest.
Arguments:
- codes: bfloat16 [4, 8, 8192, 1024], P('ckpt', 'wide'), may hold values from -4 to 4
- scales: float32 [4, 8, 8192, 8], P('ckpt', 'wide'), may hold values from 0.5 to 5
- example_ids: int32 [8, 8192], P('wide'), may hold values from 0 to 8191, each once within a row
- targets: bfloat16 [1024, 4096], P('wide'), may hold values from -0.09375 to 0.09375
- owners: int32 [6], replicated, may hold values from 0 to 7, as said below
Outputs:
- scores: float32 [8, 8192, 768], P('wide', 'ckpt')
Inputs may be any that keep to these rules, and one draw needn't show every extreme that they name: `example_ids`: each row is a permutation of the 8192 examples of its group. Distinct owners; owner 0 and owner 8 - 1 are always among them.
All inputs are finite; a program needn't handle non-finite values.
Results may differ from a plain program's by a relative error of at most 0.0029.
Values may be sent and summed in bfloat16 or wider, within the bound.
A program may use at most 192 MiB of HBM per device.

v0:
```python
import jax
import jax.numpy as jnp
from jax import lax
from jax.sharding import PartitionSpec as P


def from_root(shard, axis, root):
    mine = lax.axis_index(axis) == root
    return lax.psum(jnp.where(mine, shard, jnp.zeros_like(shard)), axis)


def fetch(targets, owner, width):
    piece = lax.dynamic_slice_in_dim(targets, lax.axis_index("ckpt") * width, width, 1)
    got = from_root(piece, "wide", owner)
    return lax.all_gather(got, "ckpt", axis=1, tiled=True)


def per_device(codes, scales, example_ids, targets, owners):
    width = codes.shape[-1]
    block = width // scales.shape[-1]
    feats = (codes[0, 0].astype(jnp.float32) * jnp.repeat(scales[0, 0], block, axis=-1)).astype(
        jnp.bfloat16
    )
    ordered = jnp.take(feats, example_ids[0], axis=0)
    rounds = owners.shape[0]
    contract = (((1,), (1,)), ((), ()))
    resident = lax.all_to_all(ordered, "ckpt", split_axis=0, concat_axis=1, tiled=True)
    columns = []
    for step in range(rounds):
        chosen = fetch(targets, owners[step], width)
        columns.append(
            lax.dot_general(resident, chosen, contract, preferred_element_type=jnp.float32)
        )
    result = jnp.concatenate(columns, axis=1)
    scale_factor = 1.0 / lax.axis_size("ckpt")
    return (result * scale_factor)[None]


def solution(mesh):
    return jax.shard_map(
        per_device,
        mesh=mesh,
        in_specs=(
            P("ckpt", "wide", None, None),
            P("ckpt", "wide", None, None),
            P("wide", None),
            P("wide", None),
            P(),
        ),
        out_specs=P("wide", "ckpt", None),
        check_vma=False,
    )
```

profile of v0, /device:TPU:28, one launch (start us, length us, event | category | flops | bytes accessed | tf_op | source)
XLA Modules:
  0.0 416.7 jit_solution(499906623515090295)
XLA Ops:
  6.5 3.5 copy.8
  10.1 0.8 compare_select_fusion
  10.9 10.3 %broadcast_in_dim.15 = f32[8192,8,128]{2,1,0:T(8,128)S(1)} broadcast(f32[8192,8]{1,0:T(8,128)} %copy.8), dimensions={0,1} | broadcast | bytes 33816576 | tf_op jit(solution)/shard_map/broadcast_in_dim | solution.py:21
  21.2 18.0 %fusion = bf16[8192,1024]{1,0:T(8,128)(2,1)} fusion(f32[1024,8,8,128]{3,2,1,0:T(8,128)S(1)} %bitcast.58, bf16[1,1,8192,1024]{3,2,1,0:T(8,128)(2,1)} %param.5), kind=kLoop, calls=%fused_computation.2 | loop fusion | flops 25165824 | bytes 67108864 | tf_op jit(solution)/shard_map/convert_element_type | solution.py:21
  39.1 48.4 %gather_fusion = bf16[8192,1024]{1,0:T(8,128)(2,1)} fusion(bf16[8192,1024]{1,0:T(8,128)(2,1)} %fusion, s32[8192]{0:T(1024)S(1)} %broadcast_clamp_fusion), kind=kCustom, calls=%fused_computation | custom fusion | bytes 33587200 | tf_op jit(solution)/shard_map/jit(_take)/gather | solution.py:24
  87.6 0.0 copy-start
  87.6 21.9 %copy.9 = bf16[4,2048,1024]{1,2,0:T(8,128)(2,1)} copy(bf16[4,2048,1024]{2,1,0:T(8,128)(2,1)} %bitcast.59) | data formatting | bytes 33554432 | tf_op jit(solution)/shard_map/jit(_take)/gather | solution.py:24
  109.5 0.5 broadcast.55
  110.0 0.0 copy-done
  110.0 0.7 reduce.3
  110.8 14.2 %broadcast_select_fusion = bf16[4,2048,1024]{1,2,0:T(8,128)(2,1)} fusion(bf16[4,2048,1024]{1,2,0:T(8,128)(2,1)} %copy.9, pred[4,2048]{1,0:T(4,128)(4,1)S(1)} %compare_and_fusion), kind=kLoop, calls=%fused_computation.3 | loop fusion | flops 8388608 | bytes 33562624 | tf_op jit(solution)/shard_map/jit(_take)/select_n | solution.py:24
  125.0 0.0 copy-start.1
  125.0 7.1 %all-to-all-start = ((bf16[4,2048,1024]{1,2,0:T(8,128)(2,1)}), bf16[4,2048,1024]{1,2,0:T(8,128)(2,1)}, u32[]{:S(2)}, u32[]{:S(2)}) async-start(bf16[4,2048,1024]{1,2,0:T(8,128)(2,1)} %broadcast_select_fusion), calls=%async_computation | async-start | bytes 33554432 | tf_op jit(solution)/shard_map/all_to_all | solution.py:27
  132.1 0.0 all-reduce.3.cloned.1.call-start
  132.1 0.0 copy-done.1
  132.1 0.7 fusion.7
  136.6 2.2 broadcast_select_fusion.1
  138.8 0.0 all-reduce.3.cloned.1.call-update
  138.8 0.0 all-gather.7.cloned.1.call-start
  138.8 89.4 %all-reduce.3.cloned.1.call-done = (bf16[128,1024]{1,0:T(8,128)(2,1)}, bf16[128,1024]{1,0:T(8,128)(2,1)}, bf16[128,1024]{1,0:T(8,128)(2,1)}, bf16[128,1024]{1,0:...) async-done(((bf16[128,1024]{1,0:T(8,128)(2,1)}, bf16[128,1024]{1,0:T(8,128)(2,1)}, bf16[128,1024]{1,0:T(8,128)(2,1)}, bf16[128,1024]{1,0:T(8,128)(2,1)}, ...) | async-done | bytes 1572880 | tf_op jit(solution)/shard_map/psum | solution.py:9
  228.2 0.0 all-gather.7.cloned.1.call-update
  228.3 0.0 all-gather.9.cloned.1.call-start
  228.3 0.7 all-gather.9.cloned.1.call-update
  229.0 0.0 all-gather.11.cloned.1.call-start
  229.0 0.5 all-gather.11.cloned.1.call-update
  229.6 0.0 all-gather.13.cloned.1.call-start
  229.6 0.5 all-gather.13.cloned.1.call-update
  230.2 0.0 all-gather.15.cloned.1.call-start
  230.2 0.5 all-gather.15.cloned.1.call-update
  230.7 0.2 all-gather.17.cloned.1.call-start
  231.0 0.5 all-gather.17.cloned.1.call-update
  231.5 21.7 %all-gather.7.cloned.1.call-done = bf16[128,4096]{1,0:T(8,128)(2,1)} async-done(((bf16[128,1024]{1,0:T(8,128)(2,1)}), bf16[128,4096]{1,0:T(8,128)(2,1)}) %all-gather.7.cloned.1.call-update) | async-done | bytes 1048592 | tf_op jit(solution)/shard_map/all_gather | solution.py:15
  253.2 86.4 %all-to-all-done = bf16[4,2048,1024]{1,2,0:T(8,128)(2,1)} async-done(((bf16[4,2048,1024]{1,2,0:T(8,128)(2,1)}), bf16[4,2048,1024]{1,2,0:T(8,128)(2,1)}, u32[]{:S(2)}, u32[]{:S(2)}) %all-to-all-start) | async-done | bytes 16777248 | tf_op jit(solution)/shard_map/all_to_all | solution.py:27
  339.6 9.5 %fusion.6 = f32[1,2048,768]{1,2,0:T(8,128)} fusion(bf16[128,4096]{1,0:T(8,128)(2,1)} %all-gather.7.cloned.1.call-done, bf16[2048,4096]{0,1:T(8,128)(2,1)} %bitcast.6), kind=kOutput, calls=%fused_computation.16 | convolution fusion | flops 2147483648 | bytes 18874368 | tf_op jit(solution)/shard_map/dot_general | solution.py:32
  349.0 0.0 all-gather.9.cloned.1.call-done
  349.0 9.8 %fusion.5 = f32[1,2048,768]{1,2,0:T(8,128)} fusion(f32[1,2048,768]{1,2,0:T(8,128)} %fusion.6, bf16[128,4096]{1,0:T(8,128)(2,1)} %all-gather.9.cloned.1.call-done, bf16[2048,4096]{0,1:T(8,128)(2,1)} %bitcast.6), kind=kOutput, calls=%fused_computation.14 | convolution fusion | flops 2147483648 | bytes 18874368 | tf_op jit(solution)/shard_map/dot_general | solution.py:32
  358.8 0.0 all-gather.11.cloned.1.call-done
  358.8 9.5 %fusion.4 = f32[1,2048,768]{1,2,0:T(8,128)} fusion(f32[1,2048,768]{1,2,0:T(8,128)} %fusion.5, bf16[128,4096]{1,0:T(8,128)(2,1)} %all-gather.11.cloned.1.call-done, bf16[2048,4096]{0,1:T(8,128)(2,1)} %bitcast.6), kind=kOutput, calls=%fused_computation.12 | convolution fusion | flops 2147483648 | bytes 18874368 | tf_op jit(solution)/shard_map/dot_general | solution.py:32
  368.3 0.0 all-gather.13.cloned.1.call-done
  368.3 9.4 %fusion.3 = f32[1,2048,768]{1,2,0:T(8,128)} fusion(f32[1,2048,768]{1,2,0:T(8,128)} %fusion.4, bf16[128,4096]{1,0:T(8,128)(2,1)} %all-gather.13.cloned.1.call-done, bf16[2048,4096]{0,1:T(8,128)(2,1)} %bitcast.6), kind=kOutput, calls=%fused_computation.10 | convolution fusion | flops 2147483648 | bytes 18874368 | tf_op jit(solution)/shard_map/dot_general | solution.py:32
  377.7 0.0 all-gather.15.cloned.1.call-done
  377.7 9.4 %fusion.2 = f32[1,2048,768]{1,2,0:T(8,128)} fusion(f32[1,2048,768]{1,2,0:T(8,128)} %fusion.3, bf16[128,4096]{1,0:T(8,128)(2,1)} %all-gather.15.cloned.1.call-done, bf16[2048,4096]{0,1:T(8,128)(2,1)} %bitcast.6), kind=kOutput, calls=%fused_computation.8 | convolution fusion | flops 2147483648 | bytes 18874368 | tf_op jit(solution)/shard_map/dot_general | solution.py:32
  387.1 0.0 all-gather.17.cloned.1.call-done
  387.1 9.7 %fusion.1 = f32[1,2048,768]{1,2,0:T(8,128)} fusion(f32[1,2048,768]{1,2,0:T(8,128)} %fusion.2, bf16[128,4096]{1,0:T(8,128)(2,1)} %all-gather.17.cloned.1.call-done, bf16[2048,4096]{0,1:T(8,128)(2,1)} %bitcast.6), kind=kOutput, calls=%fused_computation.6 | convolution fusion | flops 2147483648 | bytes 18874368 | tf_op jit(solution)/shard_map/dot_general | solution.py:32
  396.8 6.6 %broadcast_multiply_fusion = f32[1,2048,768]{1,2,0:T(8,128)} fusion(f32[1,2048,768]{1,2,0:T(8,128)} %fusion.1), kind=kLoop, calls=%fused_computation.4 | loop fusion | flops 1572864 | bytes 12582912 | tf_op jit(solution)/shard_map/mul | solution.py:36
  403.3 6.6 %copy.10 = f32[1,2048,768]{2,1,0:T(8,128)} copy(f32[1,2048,768]{1,2,0:T(8,128)} %broadcast_multiply_fusion) | data formatting | bytes 12582912 | tf_op jit(solution)/shard_map/mul | solution.py:36
  (3 shorter events, 0.0 us)
Async XLA Ops:
  87.6 22.4 %copy-start = (s32[1,8192]{1,0:T(1,128)S(1)}, s32[1,8192]{1,0:T(1,128)}, u32[]{:S(2)}) copy-start(s32[1,8192]{1,0:T(1,128)} %param.7) | copy-start | bytes 98308
  125.0 7.2 %copy-start.1 = (s32[6]{0:T(128)S(1)}, s32[6]{0:T(128)}, u32[]{:S(2)}) copy-start(s32[6]{0:T(128)} %param.9) | copy-start | bytes 76
  125.0 214.6 %all-to-all-start = ((bf16[4,2048,1024]{1,2,0:T(8,128)(2,1)}), bf16[4,2048,1024]{1,2,0:T(8,128)(2,1)}, u32[]{:S(2)}, u32[]{:S(2)}) async-start(bf16[4,2048,1024]{1,2,0:T(8,128)(2,1)} %broadcast_select_fusion), calls=%async_computation | async-start | bytes 33554432 | tf_op jit(solution)/shard_map/all_to_all | solution.py:27
  132.1 96.2 %all-reduce.3.cloned.1.call-start = ((), (), s32[]{:S(2)}) async-start(), calls=%async_computation.7 | async-start | bytes 3145728 | tf_op jit(solution)/shard_map/psum | solution.py:9
  138.8 114.4 %all-gather.7.cloned.1.call-start = ((), (), s32[]{:S(2)}) async-start(), calls=%async_computation.1 | async-start | bytes 1310720 | tf_op jit(solution)/shard_map/all_gather | solution.py:15
  228.3 120.8 %all-gather.9.cloned.1.call-start = ((), (), s32[]{:S(2)}) async-start(), calls=%async_computation.2 | async-start | bytes 1310720 | tf_op jit(solution)/shard_map/all_gather | solution.py:15
  229.0 129.8 %all-gather.11.cloned.1.call-start = ((), (), s32[]{:S(2)}) async-start(), calls=%async_computation.3 | async-start | bytes 1310720 | tf_op jit(solution)/shard_map/all_gather | solution.py:15
  229.6 138.7 %all-gather.13.cloned.1.call-start = ((), (), s32[]{:S(2)}) async-start(), calls=%async_computation.4 | async-start | bytes 1310720 | tf_op jit(solution)/shard_map/all_gather | solution.py:15
  230.2 147.5 %all-gather.15.cloned.1.call-start = ((), (), s32[]{:S(2)}) async-start(), calls=%async_computation.5 | async-start | bytes 1310720 | tf_op jit(solution)/shard_map/all_gather | solution.py:15
  230.7 156.4 %all-gather.17.cloned.1.call-start = ((), (), s32[]{:S(2)}) async-start(), calls=%async_computation.6 | async-start | bytes 1310720 | tf_op jit(solution)/shard_map/all_gather | solution.py:15
Sparse Core Ops, SparseCore 0:
  138.9 89.2 all-reduce.2
  229.8 23.3 all-gather.6
  254.8 22.4 all-gather.8
  278.6 22.4 all-gather.10
  302.5 22.3 all-gather.12
  326.3 18.1 all-gather.14
  346.1 16.6 all-gather.16
where the time goes:
time: 418 us; the launch traced here: 417 us
  waiting for transfers between devices  200 us (48%)
  local copies, waits for them, and re-layouts  91.9 us (22%)
  matrix products  57.2 us (14%)
  other arithmetic  42.4 us (10%)
  between operations  17.3 us (4%)
  starting transfers between devices  7.55 us (2%)
    psum x1, waiting for transfers between devices, from_root(): return lax.psum(jnp.where(mine, shard, jnp.zeros_like(shard)), axis)  89.4 us
    all_to_all x1, waiting for transfers between devices, per_device(): lax.all_to_all(ordered, 'ckpt', split_axis=0, concat_axis=1, tiled=True)  86.4 us
    gather x2, local copies, waits for them, and re-layouts, per_device(): ordered = jnp.take(feats, example_ids[0], axis=0)  70.4 us
    dot_general x6, matrix products, per_device(): lax.dot_general(resident, chosen, contract, preferred_element_type=jnp.fl...  57.2 us
    all_gather x6, waiting for transfers between devices, fetch(): return lax.all_gather(got, 'ckpt', axis=1, tiled=True)  21.7 us
    convert_element_type x1, other arithmetic, per_device(): (codes[0, 0].astype(jnp.float32) * jnp.repeat(scales[0, 0], block, axis=-...  18 us
    select_n x2, other arithmetic, per_device(): ordered = jnp.take(feats, example_ids[0], axis=0)  15 us
    broadcast_in_dim x1, local copies, waits for them, and re-layouts, per_device(): jnp.repeat(scales[0, 0], block, axis=-1)  10.3 us
  transfers between devices with their start and end apart: 8, of which 3 were waited for; matrix products, arithmetic and copies ran while one was open for 12% of the time, Pallas kernels for 0%

commit v1 on v0

--- a/solution.py
+++ b/solution.py
@@ -2,6 +2,22 @@
 import jax.numpy as jnp
 from jax import lax
 from jax.sharding import PartitionSpec as P
+
+
+def pairwise_exchange(x, axis, split, join):
+    ways, here = (lax.axis_size(axis), lax.axis_index(axis))
+    width = x.shape[split] // ways
+    shape = list(x.shape)
+    shape[split] = width
+    height = shape[join]
+    shape[join] = height * ways
+    full = jnp.zeros(shape, x.dtype)
+    for mask in range(ways):
+        part = lax.dynamic_slice_in_dim(x, (here ^ mask) * width, width, axis=split)
+        if mask:
+            part = lax.ppermute(part, axis, [(d, d ^ mask) for d in range(ways)])
+        full = lax.dynamic_update_slice_in_dim(full, part, (here ^ mask) * height, axis=join)
+    return full
 
 
 def from_root(shard, axis, root):
@@ -24,7 +40,7 @@
     ordered = jnp.take(feats, example_ids[0], axis=0)
     rounds = owners.shape[0]
     contract = (((1,), (1,)), ((), ()))
-    resident = lax.all_to_all(ordered, "ckpt", split_axis=0, concat_axis=1, tiled=True)
+    resident = pairwise_exchange(ordered, "ckpt", 0, 1)
     columns = []
     for step in range(rounds):
         chosen = fetch(targets, owners[step], width)

time: 418 us -> 489 us (1.17)
  waiting for transfers between devices: 200 us -> 245 us
  matrix products: 57.2 us -> 75.9 us
  local copies, waits for them, and re-layouts: 91.9 us -> 102 us
  starting transfers between devices: 7.55 us -> 2.29 us
    ppermute x0 -> x3, waiting for transfers between devices: none -> 187 us  [pairwise_exchange(): part = lax.ppermute(part, axis, [(d, d ^ mask) for d in range(ways)])]
    all_to_all x1 -> x0, waiting for transfers between devices: 86.4 us -> none  [per_device(): lax.all_to_all(ordered, 'ckpt', split_axis=0, concat_axis=1, tiled=True)]
    psum x1, waiting for transfers between devices: 89.4 us -> 57.1 us  [from_root(): return lax.psum(jnp.where(mine, shard, jnp.zeros_like(shard)), axis)]
    all_gather x6, waiting for transfers between devices: 21.7 us -> 0.01 us  [fetch(): return lax.all_gather(got, 'ckpt', axis=1, tiled=True)]
    gather x2 -> x1, local copies, waits for them, and re-layouts: 70.4 us -> 48.7 us  [per_device(): ordered = jnp.take(feats, example_ids[0], axis=0)]
    dot_general x6, matrix products: 57.2 us -> 75.9 us  [per_device(): lax.dot_general(resident, chosen, contract, preferred_element_type=jnp.fl...]
    dynamic_update_slice x0 -> x3, local copies, waits for them, and re-layouts: none -> 13.9 us  [pairwise_exchange(): lax.dynamic_update_slice_in_dim(full, part, (here ^ mask) * height, axis=...]
    broadcast_in_dim x0 -> x1, local copies, waits for them, and re-layouts: none -> 8.37 us  [pairwise_exchange(): full = jnp.zeros(shape, x.dtype)]
  transfers between devices with their start and end apart: 8 -> 10, of which waited for: 3 -> 4; matrix products, arithmetic and copies ran while one was open for 12% -> 39% of each run, Pallas kernels for 0% -> 0%
where the time goes in v1:
time: 489 us; the launch traced here: 484 us
  waiting for transfers between devices  245 us (50%)
  local copies, waits for them, and re-layouts  102 us (21%)
  matrix products  75.9 us (16%)
  other arithmetic  41.1 us (8%)
  between operations  17.4 us (4%)
    ppermute x3, waiting for transfers between devices, pairwise_exchange(): part = lax.ppermute(part, axis, [(d, d ^ mask) for d in range(ways)])  187 us
    dot_general x6, matrix products, per_device(): lax.dot_general(resident, chosen, contract, preferred_element_type=jnp.fl...  75.9 us
    psum x1, waiting for transfers between devices, from_root(): return lax.psum(jnp.where(mine, shard, jnp.zeros_like(shard)), axis)  57.1 us
    gather x1, local copies, waits for them, and re-layouts, per_device(): ordered = jnp.take(feats, example_ids[0], axis=0)  48.7 us
    convert_element_type x1, other arithmetic, per_device(): (codes[0, 0].astype(jnp.float32) * jnp.repeat(scales[0, 0], block, axis=-...  18 us
    select_n x2, other arithmetic, per_device(): ordered = jnp.take(feats, example_ids[0], axis=0)  14.3 us
    dynamic_update_slice x3, local copies, waits for them, and re-layouts, pairwise_exchange(): lax.dynamic_update_slice_in_dim(full, part, (here ^ mask) * height, axis=...  13.9 us
    broadcast_in_dim x1, local copies, waits for them, and re-layouts, per_device(): jnp.repeat(scales[0, 0], block, axis=-1)  10.3 us
  transfers between devices with their start and end apart: 10, of which 4 were waited for; matrix products, arithmetic and copies ran while one was open for 39% of the time, Pallas kernels for 0%

profile of v1, /device:TPU:28, one launch (start us, length us, event | category | flops | bytes accessed | tf_op | source)
XLA Modules:
  0.0 484.3 jit_solution(1727324952885623996)
XLA Ops:
  6.5 0.0 all-reduce.3.cloned.1.call-start
  6.5 1.6 fusion.7
  11.9 2.2 broadcast_select_fusion.1
  14.1 0.0 all-reduce.3.cloned.1.call-update
  14.2 0.0 all-gather.7.cloned.1.call-start
  14.2 3.5 copy.8
  17.7 10.3 %broadcast_in_dim.19 = f32[8192,8,128]{2,1,0:T(8,128)S(1)} broadcast(f32[8192,8]{1,0:T(8,128)} %copy.8), dimensions={0,1} | broadcast | bytes 33816576 | tf_op jit(solution)/shard_map/broadcast_in_dim | solution.py:37
  28.0 0.0 copy-start.1
  28.0 18.0 %fusion = bf16[8192,1024]{1,0:T(8,128)(2,1)} fusion(f32[1024,8,8,128]{3,2,1,0:T(8,128)S(1)} %bitcast.55, bf16[1,1,8192,1024]{3,2,1,0:T(8,128)(2,1)} %param.5), kind=kLoop, calls=%fused_computation.2 | loop fusion | flops 25165824 | bytes 67108864 | tf_op jit(solution)/shard_map/convert_element_type | solution.py:37
  46.1 57.1 %all-reduce.3.cloned.1.call-done = (bf16[128,1024]{1,0:T(8,128)(2,1)}, bf16[128,1024]{1,0:T(8,128)(2,1)}, bf16[128,1024]{1,0:T(8,128)(2,1)}, bf16[128,1024]{1,0:...) async-done(((bf16[128,1024]{1,0:T(8,128)(2,1)}, bf16[128,1024]{1,0:T(8,128)(2,1)}, bf16[128,1024]{1,0:T(8,128)(2,1)}, bf16[128,1024]{1,0:T(8,128)(2,1)}, ...) | async-done | bytes 1572880 | tf_op jit(solution)/shard_map/psum | solution.py:25
  103.2 0.0 all-gather.7.cloned.1.call-update
  103.2 0.0 all-gather.9.cloned.1.call-start
  103.3 0.0 copy-done.1
  103.3 48.7 %gather_fusion = bf16[8192,1024]{1,0:T(8,128)(2,1)} fusion(bf16[8192,1024]{1,0:T(8,128)(2,1)} %fusion, s32[8192]{0:T(1024)S(1)} %broadcast_clamp_fusion), kind=kCustom, calls=%fused_computation | custom fusion | bytes 33587200 | tf_op jit(solution)/shard_map/jit(_take)/gather | solution.py:40
  152.0 0.0 all-gather.9.cloned.1.call-update
  152.1 0.0 all-gather.11.cloned.1.call-start
  152.1 14.3 %broadcast_select_fusion = bf16[8192,1024]{1,0:T(8,128)(2,1)} fusion(bf16[8192,1024]{1,0:T(8,128)(2,1)} %gather_fusion, pred[8192]{0:T(1024)(128)(4,1)S(1)} %compare_and_fusion), kind=kLoop, calls=%fused_computation.3 | loop fusion | flops 8388608 | bytes 33562624 | tf_op jit(solution)/shard_map/jit(_take)/select_n | solution.py:40
  166.4 0.0 all-gather.11.cloned.1.call-update
  166.4 0.0 all-gather.13.cloned.1.call-start
  166.4 0.0 copy-start
  166.5 8.4 %broadcast_in_dim.17 = bf16[2048,4096]{1,0:T(8,128)(2,1)} broadcast(bf16[]{:T(256)} %constant.14.clone.1), dimensions={} | broadcast | bytes 16777218 | tf_op jit(solution)/shard_map/broadcast_in_dim | solution.py:14
  174.8 3.1 copy-done
  178.0 6.1 %constant_dynamic-slice_fusion = (bf16[2048,1024]{1,0:T(8,128)(2,1)}, bf16[2048,1024]{1,0:T(8,128)(2,1)}, bf16[2048,1024]{1,0:T(8,128)(2,1)}, bf16[2048,4096]{1,0:T(8,128)(2,1)}) fusion(bf16[8192,1024]{1,0:T(8,128)(2,1)S(1)} %copy-done, s32[]{:T(128)S(6)} %select_n.97, s32[]{:T(128)S(6)} %select_n.95, s32[]{:T(128)S(6)} %select_n.93, ...), kind=kLoop, calls=%fused_computation.29 | loop fusion | bytes 33554452 | tf_op jit(solution)/shard_map/dynamic_slice | solution.py:16
  184.1 0.0 collective-permute-start
  184.1 1.5 collective-permute-start.1
  185.6 0.3 collective-permute-start.2
  185.9 0.0 all-gather.13.cloned.1.call-update
  186.0 0.0 all-gather.15.cloned.1.call-start
  186.0 0.5 all-gather.15.cloned.1.call-update
  186.5 0.2 all-gather.17.cloned.1.call-start
  186.8 0.5 all-gather.17.cloned.1.call-update
  187.3 4.4 collective-permute-done
  191.7 4.6 constant_dynamic-update-slice_fusion.2
  196.3 98.4 %collective-permute-done.1 = bf16[2048,1024]{1,0:T(8,128)(2,1)} collective-permute-done((bf16[2048,1024]{1,0:T(8,128)(2,1)}, bf16[2048,1024]{1,0:T(8,128)(2,1)}, u32[]{:S(2)}, u32[]{:S(2)}) %collective-permute-start.1) | collective-permute-done | bytes 4194336 | tf_op jit(solution)/shard_map/ppermute | solution.py:18
  294.7 4.6 constant_dynamic-update-slice_fusion.1
  299.3 84.4 %collective-permute-done.2 = bf16[2048,1024]{1,0:T(8,128)(2,1)} collective-permute-done((bf16[2048,1024]{1,0:T(8,128)(2,1)}, bf16[2048,1024]{1,0:T(8,128)(2,1)}, u32[]{:S(2)}, u32[]{:S(2)}) %collective-permute-start.2) | collective-permute-done | bytes 4194336 | tf_op jit(solution)/shard_map/ppermute | solution.py:18
  383.7 4.7 constant_dynamic-update-slice_fusion
  388.4 0.0 all-gather.7.cloned.1.call-done
  388.4 12.6 %fusion.6 = f32[1,2048,768]{1,2,0:T(8,128)} fusion(bf16[2048,4096]{1,0:T(8,128)(2,1)} %constant_dynamic-update-slice_fusion, bf16[128,4096]{1,0:T(8,128)(2,1)} %all-gather.7.cloned.1.call-done), kind=kOutput, calls=%fused_computation.17 | convolution fusion | flops 2147483648 | bytes 18874368 | tf_op jit(solution)/shard_map/dot_general | solution.py:48
  401.0 0.0 all-gather.9.cloned.1.call-done
  401.0 12.6 %fusion.5 = f32[1,2048,768]{1,2,0:T(8,128)} fusion(f32[1,2048,768]{1,2,0:T(8,128)} %fusion.6, bf16[2048,4096]{1,0:T(8,128)(2,1)} %constant_dynamic-update-slice_fusion, bf16[128,4096]{1,0:T(8,128)(2,1)} %all-gather.9.cloned.1.call-done), kind=kOutput, calls=%fused_computation.15 | convolution fusion | flops 2147483648 | bytes 18874368 | tf_op jit(solution)/shard_map/dot_general | solution.py:48
  413.6 0.0 all-gather.11.cloned.1.call-done
  413.6 12.8 %fusion.4 = f32[1,2048,768]{1,2,0:T(8,128)} fusion(f32[1,2048,768]{1,2,0:T(8,128)} %fusion.5, bf16[2048,4096]{1,0:T(8,128)(2,1)} %constant_dynamic-update-slice_fusion, bf16[128,4096]{1,0:T(8,128)(2,1)} %all-gather.11.cloned.1.call-done), kind=kOutput, calls=%fused_computation.13 | convolution fusion | flops 2147483648 | bytes 18874368 | tf_op jit(solution)/shard_map/dot_general | solution.py:48
  426.4 0.0 all-gather.13.cloned.1.call-done
  426.4 12.6 %fusion.3 = f32[1,2048,768]{1,2,0:T(8,128)} fusion(f32[1,2048,768]{1,2,0:T(8,128)} %fusion.4, bf16[2048,4096]{1,0:T(8,128)(2,1)} %constant_dynamic-update-slice_fusion, bf16[128,4096]{1,0:T(8,128)(2,1)} %all-gather.13.cloned.1.call-done), kind=kOutput, calls=%fused_computation.11 | convolution fusion | flops 2147483648 | bytes 18874368 | tf_op jit(solution)/shard_map/dot_general | solution.py:48
  439.0 0.0 all-gather.15.cloned.1.call-done
  439.0 12.6 %fusion.2 = f32[1,2048,768]{1,2,0:T(8,128)} fusion(f32[1,2048,768]{1,2,0:T(8,128)} %fusion.3, bf16[2048,4096]{1,0:T(8,128)(2,1)} %constant_dynamic-update-slice_fusion, bf16[128,4096]{1,0:T(8,128)(2,1)} %all-gather.15.cloned.1.call-done), kind=kOutput, calls=%fused_computation.9 | convolution fusion | flops 2147483648 | bytes 18874368 | tf_op jit(solution)/shard_map/dot_general | solution.py:48
  451.7 0.0 all-gather.17.cloned.1.call-done
  451.7 12.6 %fusion.1 = f32[1,2048,768]{1,2,0:T(8,128)} fusion(f32[1,2048,768]{1,2,0:T(8,128)} %fusion.2, bf16[2048,4096]{1,0:T(8,128)(2,1)} %constant_dynamic-update-slice_fusion, bf16[128,4096]{1,0:T(8,128)(2,1)} %all-gather.17.cloned.1.call-done), kind=kOutput, calls=%fused_computation.7 | convolution fusion | flops 2147483648 | bytes 18874368 | tf_op jit(solution)/shard_map/dot_general | solution.py:48
  464.3 6.6 %broadcast_multiply_fusion = f32[1,2048,768]{1,2,0:T(8,128)} fusion(f32[1,2048,768]{1,2,0:T(8,128)} %fusion.1), kind=kLoop, calls=%fused_computation.5 | loop fusion | flops 1572864 | bytes 12582912 | tf_op jit(solution)/shard_map/mul | solution.py:52
  470.8 6.6 %copy.9 = f32[1,2048,768]{2,1,0:T(8,128)} copy(f32[1,2048,768]{1,2,0:T(8,128)} %broadcast_multiply_fusion) | data formatting | bytes 12582912 | tf_op jit(solution)/shard_map/mul | solution.py:52
  (3 shorter events, 0.1 us)
Async XLA Ops:
  6.5 96.7 %all-reduce.3.cloned.1.call-start = ((), (), s32[]{:S(2)}) async-start(), calls=%async_computation.6 | async-start | bytes 3145728 | tf_op jit(solution)/shard_map/psum | solution.py:25
  14.2 374.2 %all-gather.7.cloned.1.call-start = ((), (), s32[]{:S(2)}) async-start(), calls=%async_computation | async-start | bytes 1310720 | tf_op jit(solution)/shard_map/all_gather | solution.py:31
  28.0 75.2 %copy-start.1 = (s32[1,8192]{1,0:T(1,128)S(1)}, s32[1,8192]{1,0:T(1,128)}, u32[]{:S(2)}) copy-start(s32[1,8192]{1,0:T(1,128)} %param.7) | copy-start | bytes 98308
  103.2 297.8 %all-gather.9.cloned.1.call-start = ((), (), s32[]{:S(2)}) async-start(), calls=%async_computation.1 | async-start | bytes 1310720 | tf_op jit(solution)/shard_map/all_gather | solution.py:31
  152.1 261.5 %all-gather.11.cloned.1.call-start = ((), (), s32[]{:S(2)}) async-start(), calls=%async_computation.2 | async-start | bytes 1310720 | tf_op jit(solution)/shard_map/all_gather | solution.py:31
  166.4 260.0 %all-gather.13.cloned.1.call-start = ((), (), s32[]{:S(2)}) async-start(), calls=%async_computation.3 | async-start | bytes 1310720 | tf_op jit(solution)/shard_map/all_gather | solution.py:31
  166.4 11.5 %copy-start = (bf16[8192,1024]{1,0:T(8,128)(2,1)S(1)}, bf16[8192,1024]{1,0:T(8,128)(2,1)}, u32[]{:S(2)}) copy-start(bf16[8192,1024]{1,0:T(8,128)(2,1)} %broadcast_select_fusion) | copy-start | bytes 50331652
  184.1 7.6 %collective-permute-start = (bf16[2048,1024]{1,0:T(8,128)(2,1)}, bf16[2048,1024]{1,0:T(8,128)(2,1)}, u32[]{:S(2)}, u32[]{:S(2)}) collective-permute-start(bf16[2048,1024]{1,0:T(8,128)(2,1)} %get-tuple-element.13), channel_id=1, source_target_pairs={{0,8},{8,0},{16,24},{24,16},{1,9},{9,1},{17,25},{25,17},{2,10},{10... | collective-permute-start | bytes 12582920 | tf_op jit(solution)/shard_map/ppermute | solution.py:18
  184.1 110.6 %collective-permute-start.1 = (bf16[2048,1024]{1,0:T(8,128)(2,1)}, bf16[2048,1024]{1,0:T(8,128)(2,1)}, u32[]{:S(2)}, u32[]{:S(2)}) collective-permute-start(bf16[2048,1024]{1,0:T(8,128)(2,1)} %get-tuple-element.12), channel_id=1, source_target_pairs={{0,16},{8,24},{16,0},{24,8},{1,17},{9,25},{17,1},{25,9},{2,18},{10... | collective-permute-start | bytes 12582920 | tf_op jit(solution)/shard_map/ppermute | solution.py:18
  185.6 198.0 %collective-permute-start.2 = (bf16[2048,1024]{1,0:T(8,128)(2,1)}, bf16[2048,1024]{1,0:T(8,128)(2,1)}, u32[]{:S(2)}, u32[]{:S(2)}) collective-permute-start(bf16[2048,1024]{1,0:T(8,128)(2,1)} %get-tuple-element.11), channel_id=1, source_target_pairs={{0,24},{8,16},{16,8},{24,0},{1,25},{9,17},{17,9},{25,1},{2,26},{10... | collective-permute-start | bytes 12582920 | tf_op jit(solution)/shard_map/ppermute | solution.py:18
  186.0 253.1 %all-gather.15.cloned.1.call-start = ((), (), s32[]{:S(2)}) async-start(), calls=%async_computation.4 | async-start | bytes 1310720 | tf_op jit(solution)/shard_map/all_gather | solution.py:31
  186.5 265.1 %all-gather.17.cloned.1.call-start = ((), (), s32[]{:S(2)}) async-start(), calls=%async_computation.5 | async-start | bytes 1310720 | tf_op jit(solution)/shard_map/all_gather | solution.py:31
Sparse Core Ops, SparseCore 0:
  14.3 88.8 all-reduce.2
  104.8 17.6 all-gather.6
  152.2 17.6 all-gather.8
  171.3 16.7 all-gather.10
  189.4 22.4 all-gather.12
  213.3 22.4 all-gather.14
  237.3 22.4 all-gather.16
